TPU v7x, 256 devices: a whole 4x4x8 slice. The times are simulated.
256 devices in a mesh: dp: 16 (over z, x_lo), seq: 16 (over y, x_hi, core).
Axes of the slice: x: 4 (x_hi: 2, x_lo: 2; x = x_hi * 2 + x_lo), y: 4, z: 8, core: 2. Of those that a mesh axis runs over, the one named last changes fastest.
Arguments:
- states: bfloat16 [16, 1024, 4096], P('dp', 'seq'), may hold values from -6 to 6
- kv_weight: bfloat16 [4096, 1536], P('seq'), may hold values from -0.09375 to 0.09375
- queries: bfloat16 [16, 4096, 768], P('dp', 'seq'), may hold values from -150 to 150
- hidden: bfloat16 [16, 4096, 1536], P('dp', 'seq'), may hold values from -3 to 3
- out_proj: bfloat16 [768, 1536], P('seq'), may hold values from -0.21875 to 0.21875
- disc_in: bfloat16 [1536, 1024], replicated, may hold values from -0.15625 to 0.15625
- conv_weight: bfloat16 [41, 64, 1024], replicated, may hold values from -0.125 to 0.125
- score_weight: float32 [1024], replicated, may hold values from -0.1875 to 0.1875
- frame_len: int32 [16], replicated, may hold values from 1024 to 4096, as said below
- state_len: int32 [16], replicated, may hold values from 256 to 1024, as said below
Outputs:
- grad_out_proj: float32 [768, 1536], P('seq')
- loss_mean: float32 [], replicated
Inputs may be any that keep to these rules, and one draw needn't show every extreme that they name: `frame_len`: one clip has all 4096 frames live in every draw. `state_len`: one clip has all 1024 backbone frames live in every draw.
All inputs are finite; a program needn't handle non-finite values.
Results may differ from a plain program's by a relative error of at most 0.005.
Values may be sent and summed in bfloat16 or wider, within the bound.
No kernel may reach another device: no remote copies, remote signals or barrier semaphores. Data moves between devices by JAX's collectives and lax.ppermute only.
A program may use at most 128 MiB of HBM per device.

v0:
```python
import math
import jax
import jax.numpy as jnp
from jax import lax
from jax.sharding import PartitionSpec as P

HEAD_DIM = 128
GROUPS = 16
STRIDE = 4


def with_halo(array, sides, width):
    for axis, dim in sides:
        size, length = (lax.axis_size(axis), array.shape[dim])
        up = [(i, (i + 1) % size) for i in range(size - 1)]
        down = [(j, i) for i, j in up]
        last = lax.slice_in_dim(array, length - width, length, axis=dim)
        initial = lax.slice_in_dim(array, 0, width, axis=dim)
        before = lax.ppermute(last, axis, up)
        after = lax.ppermute(initial, axis, down)
        array = jnp.concatenate([before, array, after], axis=dim)
    return array


def regroup(weight_taps, group_count):
    kernel, group_in, channels = weight_taps.shape
    blocks = weight_taps.reshape(kernel, group_in, group_count, channels // group_count)
    turned = jnp.transpose(blocks, (0, 3, 2, 1)).reshape(kernel, channels // group_count, channels)
    return jnp.flip(turned, 0)


def disc_conv(padded, weight_taps, group_count, stride):
    return lax.conv_general_dilated(
        padded[None],
        weight_taps,
        (stride,),
        "VALID",
        dimension_numbers=("NWC", "WIO", "NWC"),
        feature_group_count=group_count,
        preferred_element_type=jnp.float32,
    )[0]


def disc_back(grad_wide, flipped, group_count, stride, high_pad):
    return lax.conv_general_dilated(
        grad_wide[None],
        flipped,
        (1,),
        [(0, high_pad)],
        lhs_dilation=(stride,),
        dimension_numbers=("NWC", "WIO", "NWC"),
        feature_group_count=group_count,
        preferred_element_type=jnp.float32,
    )[0]


def attend(query, keys_values, live_keys):
    row_count, att_width = query.shape
    head_count = att_width // HEAD_DIM
    query_heads = query.astype(jnp.float32).reshape(row_count, head_count, HEAD_DIM)
    key_heads = keys_values[:, :att_width].reshape(-1, head_count, HEAD_DIM)
    value_heads = keys_values[:, att_width:].reshape(-1, head_count, HEAD_DIM)
    scores = jnp.einsum(
        "qhd,khd->hqk", query_heads, key_heads, precision=lax.Precision.HIGHEST
    ) / math.sqrt(HEAD_DIM)
    scores = jnp.where(live_keys[None, None, :], scores, -1e30)
    row_max = jnp.max(scores, axis=2, keepdims=True)
    expo_scores = jnp.where(live_keys[None, None, :], jnp.exp(scores - row_max), 0.0)
    denom = jnp.sum(expo_scores, axis=2)
    weights = expo_scores.astype(jnp.bfloat16)
    mixed_heads = jnp.einsum(
        "hqk,khd->qhd", weights.astype(jnp.float32), value_heads, precision=lax.Precision.HIGHEST
    )
    mixed_heads = mixed_heads / jnp.transpose(denom)[:, :, None]
    return mixed_heads.reshape(row_count, att_width).astype(jnp.bfloat16)


def shards(
    states,
    kv_weight,
    queries,
    hidden,
    out_proj,
    disc_in,
    conv_weight,
    score_weight,
    frame_len,
    state_len,
):
    states_local = states[0]
    frame_count = hidden.shape[1]
    clip_index = lax.axis_index("dp")
    seq_index = lax.axis_index("seq")
    clip_pick = jnp.arange(frame_len.shape[0]) == clip_index
    clip_frames = jnp.sum(jnp.where(clip_pick, frame_len, 0))
    clip_states = jnp.sum(jnp.where(clip_pick, state_len, 0))
    sliced = states_local
    projected = jnp.dot(
        sliced,
        lax.all_gather(kv_weight, "seq", axis=0, tiled=True),
        preferred_element_type=jnp.float32,
    )
    keys_values = lax.all_gather(projected, "seq", axis=0, tiled=True)
    live_keys = jnp.arange(keys_values.shape[0]) < clip_states
    attended = attend(queries[0], keys_values, live_keys)
    sliced = attended
    lifted = hidden[0].astype(jnp.float32) + jnp.dot(
        sliced,
        lax.all_gather(out_proj, "seq", axis=0, tiled=True),
        preferred_element_type=jnp.float32,
    )
    mixed_rows = lifted.astype(jnp.bfloat16)
    frame_ids = seq_index * frame_count + jnp.arange(frame_count)
    inside = (frame_ids < clip_frames)[:, None]
    disc_feed = jnp.where(
        inside, jnp.dot(mixed_rows, disc_in, preferred_element_type=jnp.float32), 0.0
    ).astype(jnp.bfloat16)
    margin_rows = (conv_weight.shape[0] - 1) // 2
    padded = with_halo(disc_feed, (("seq", 0),), margin_rows)
    pre = disc_conv(padded, conv_weight, GROUPS, STRIDE)
    sigmoid_pre = jax.nn.sigmoid(pre)
    critic = jnp.dot(pre * sigmoid_pre, score_weight, precision=lax.Precision.HIGHEST)
    out_count = pre.shape[0]
    valid_out = STRIDE * (seq_index * out_count + jnp.arange(out_count)) < clip_frames
    shortfall = 1.0 - critic
    local_loss = jnp.sum(jnp.where(valid_out, shortfall * shortfall, 0.0))
    push_score = jnp.where(valid_out, -2.0 * shortfall, 0.0)
    slope_pre = sigmoid_pre * (1.0 + pre * (1.0 - sigmoid_pre))
    grad_pre = (push_score[:, None] * score_weight[None, :] * slope_pre).astype(jnp.bfloat16)
    reach_out = margin_rows // STRIDE
    grad_wide = with_halo(grad_pre, (("seq", 0),), reach_out)
    grad_feed = disc_back(grad_wide, regroup(conv_weight, GROUPS), GROUPS, STRIDE, STRIDE - 1)
    grad_feed = jnp.where(inside, grad_feed, 0.0).astype(jnp.bfloat16)
    grad_mixed = lax.dot_general(
        grad_feed, disc_in, (((1,), (1,)), ((), ())), preferred_element_type=jnp.float32
    ).astype(jnp.bfloat16)
    full_term = lax.dot_general(
        attended, grad_mixed, (((0,), (0,)), ((), ())), preferred_element_type=jnp.float32
    )
    summed_clips = lax.psum(full_term, "dp")
    grad_proj = lax.psum_scatter(summed_clips, "seq", scatter_dimension=0, tiled=True)
    total_loss = lax.psum(local_loss, ("dp", "seq"))
    counted = jnp.sum((frame_len + STRIDE - 1) // STRIDE).astype(jnp.float32)
    return (grad_proj, total_loss / counted)


def solution(mesh):
    return jax.shard_map(
        shards,
        mesh=mesh,
        in_specs=(
            P("dp", "seq", None),
            P("seq", None),
            P("dp", "seq", None),
            P("dp", "seq", None),
            P("seq", None),
            P(),
            P(),
            P(),
            P(),
            P(),
        ),
        out_specs=(P("seq", None), P()),
        check_vma=False,
    )
```

profile of v0, /device:TPU:8, one launch (start us, length us, event | category | flops | bytes accessed | tf_op | source)
XLA Modules:
  0.0 666.0 jit_solution(14477105413284666974)
XLA Ops:
  7.2 0.0 copy-start
  7.2 0.0 all-gather.4.cloned.1.call-start
  7.2 0.7 all-gather.4.cloned.1.call-update
  7.9 0.0 copy-start.7
  7.9 0.0 copy-start.8
  7.9 0.0 all-gather.6.cloned.1.call-start
  8.0 100.1 %all-gather.4.cloned.1.call-done = bf16[4096,1536]{1,0:T(8,128)(2,1)} async-done(((bf16[256,1536]{1,0:T(8,128)(2,1)}), bf16[4096,1536]{1,0:T(8,128)(2,1)}) %all-gather.4.cloned.1.call-update) | async-done | bytes 12582928 | tf_op jit(solution)/shard_map/all_gather | solution.py:100
  108.1 7.8 %fusion.31 = f32[64,1536]{1,0:T(8,128)} fusion(bf16[4096,1536]{1,0:T(8,128)(2,1)} %all-gather.4.cloned.1.call-done, bf16[1,64,4096]{2,1,0:T(8,128)(2,1)} %param.10), kind=kOutput, calls=%fused_computation.30 | convolution fusion | flops 805306368 | bytes 13500416 | tf_op jit(solution)/shard_map/dot_general | solution.py:98
  115.8 0.0 all-gather.6.cloned.1.call-update
  115.9 0.0 all-gather.8.cloned.1.call-start
  115.9 0.7 all-gather.8.cloned.1.call-update
  116.6 0.0 reduce-scatter.2.cloned.1.call-start
  116.7 1.2 copy.20
  117.8 0.0 copy-done.7
  117.8 0.0 copy-done.8
  117.8 0.7 fusion.42
  118.6 0.7 add_compare_fusion
  119.2 0.0 copy-start.5
  119.2 0.7 iota_compare_fusion
  119.9 63.1 %all-gather.6.cloned.1.call-done = f32[1024,1536]{1,0:T(8,128)} async-done(((f32[64,1536]{1,0:T(8,128)}), f32[1024,1536]{1,0:T(8,128)}) %all-gather.6.cloned.1.call-update) | async-done | bytes 6291472 | tf_op jit(solution)/shard_map/all_gather | solution.py:103
  183.0 5.9 fusion.48
  188.9 3.5 copy.19
  192.5 3.6 copy.18
  196.0 4.6 fusion.52
  200.6 0.0 copy-start.1
  200.6 2.4 fusion.51
  203.1 1.7 fusion.24
  204.8 33.3 %all-gather.8.cloned.1.call-done = bf16[768,1536]{1,0:T(8,128)(2,1)} async-done(((bf16[48,1536]{1,0:T(8,128)(2,1)}), bf16[768,1536]{1,0:T(8,128)(2,1)}) %all-gather.8.cloned.1.call-update) | async-done | bytes 2359312 | tf_op jit(solution)/shard_map/all_gather | solution.py:109
  238.1 4.3 fusion.23
  242.4 1.5 fusion.49
  243.8 2.2 collective-permute-start
  246.0 5.8 collective-permute-start.1
  251.8 14.8 %shard_map.115 = bf16[41,64,16,64]{3,2,1,0:T(8,128)(2,1)} reshape(bf16[41,64,1024]{2,1,0:T(8,128)(2,1)} %param.16) | data formatting | bytes 10747904 | tf_op jit(solution)/shard_map/shard_map
  266.6 0.0 collective-permute-done
  266.6 0.0 collective-permute-done.1
  266.6 2.0 pad_maximum_fusion
  268.6 2.3 copy.24
  270.9 6.3 copy.25
  277.2 0.0 copy-start.4
  277.2 18.9 %fusion.27 = f32[64,16,64]{2,1,0:T(8,128)} fusion(bf16[1,296,16,64]{3,0,2,1:T(2,128)(2,1)} %copy.25, bf16[41,64,16,64]{3,2,1,0:T(8,128)(2,1)} %shard_map.115), kind=kOutput, calls=%fused_computation.25 | convolution fusion | flops 343932928 | bytes 6242304 | tf_op jit(solution)/shard_map/conv_general_dilated | solution.py:33
  296.1 1.2 squeeze.12
  297.3 1.6 fusion.41
  298.9 0.1 multiply_convert_fusion
  299.1 1.9 collective-permute-start.2
  301.0 6.0 collective-permute-start.3
  307.1 19.1 %copy.27 = bf16[41,64,16,64]{1,2,3,0:T(8,128)(2,1)} copy(bf16[41,64,16,64]{3,2,1,0:T(8,128)(2,1)} %shard_map.115) | data formatting | bytes 10747904 | tf_op jit(solution)/shard_map/shard_map
  326.2 15.0 %reshape.48 = bf16[41,64,1024]{2,1,0:T(8,128)(2,1)} reshape(bf16[41,64,16,64]{3,2,1,0:T(8,128)(2,1)} %bitcast.55) | data formatting | bytes 10747904 | tf_op jit(solution)/shard_map/reshape | solution.py:28
  341.2 5.9 rev.6
  347.1 14.8 %rev.7 = bf16[41,64,16,64]{3,2,1,0:T(8,128)(2,1)} reshape(bf16[41,64,1024]{2,1,0:T(8,128)(2,1)} %rev.6) | data formatting | bytes 10747904 | tf_op jit(solution)/shard_map/jit(_flip)/rev | solution.py:29
  361.9 0.0 collective-permute-done.2
  361.9 0.0 collective-permute-done.3
  362.0 1.2 broadcast_in_dim.69
  363.2 54.6 %fusion.1 = bf16[1,256,16,64]{3,0,2,1:T(2,128)(2,1)} fusion(bf16[1,74,16,64]{3,0,2,1:T(2,128)(2,1)} %broadcast_in_dim.69, bf16[41,64,16,64]{3,2,1,0:T(8,128)(2,1)} %rev.7), kind=kOutput, calls=%fused_computation.1 | convolution fusion | flops 343932928 | bytes 6049792 | tf_op jit(solution)/shard_map/conv_general_dilated | solution.py:45
  417.8 5.7 copy.30
  423.5 2.1 copy.31
  425.5 0.0 copy-done.6
  425.5 4.8 fusion.16
  430.3 0.0 reduce-scatter.2.cloned.1.call-update
  430.4 0.0 all-reduce.2.cloned.1.call-start
  430.4 88.9 %reduce-scatter.2.cloned.1.call-done = f32[48,1536]{1,0:T(8,128)} async-done(((f32[768,1536]{1,0:T(8,128)}), f32[48,1536]{1,0:T(8,128)}) %reduce-scatter.2.cloned.1.call-update) | async-done | bytes 294928 | tf_op jit(solution)/shard_map/reduce_scatter | solution.py:141
  519.3 0.0 all-reduce.2.cloned.1.call-update
  520.0 74.0 %psum.15 = f32[]{:T(128)} all-reduce(f32[]{:T(128)} %get-tuple-element.10), channel_id=1, replica_groups=mesh['dp'=16,'seq'=16] {'dp','seq'}, use_global_device_ids=true, to_apply=%region_7.8 | all-reduce | flops 1 | bytes 8 | tf_op jit(solution)/shard_map/psum | solution.py:142
  594.7 61.6 %all-reduce.2.cloned.1.call-done = f32[48,1536]{1,0:T(8,128)} async-done(((f32[48,1536]{1,0:T(8,128)}), f32[48,1536]{1,0:T(8,128)}) %all-reduce.2.cloned.1.call-update) | async-done | bytes 294928 | tf_op jit(solution)/shard_map/psum | solution.py:140
  656.3 1.7 copy.42
  (11 shorter events, 0.1 us)
Async XLA Ops:
  7.2 231.0 %copy-start = (bf16[1536,1024]{1,0:T(8,128)(2,1)S(1)}, bf16[1536,1024]{1,0:T(8,128)(2,1)}, u32[]{:S(2)}) copy-start(bf16[1536,1024]{1,0:T(8,128)(2,1)} %param.15) | copy-start | bytes 9437188
  7.2 100.9 %all-gather.4.cloned.1.call-start = ((), (), s32[]{:S(2)}) async-start(), calls=%async_computation.1 | async-start | bytes 13369344 | tf_op jit(solution)/shard_map/all_gather | solution.py:100
  7.9 109.9 %copy-start.7 = (s32[16]{0:T(128)S(1)}, s32[16]{0:T(128)}, u32[]{:S(2)}) copy-start(s32[16]{0:T(128)} %param.18) | copy-start | bytes 196
  7.9 109.9 %copy-start.8 = (s32[16]{0:T(128)S(1)}, s32[16]{0:T(128)}, u32[]{:S(2)}) copy-start(s32[16]{0:T(128)} %param.19) | copy-start | bytes 196
  7.9 175.1 %all-gather.6.cloned.1.call-start = ((), (), s32[]{:S(2)}) async-start(), calls=%async_computation.2 | async-start | bytes 6684672 | tf_op jit(solution)/shard_map/all_gather | solution.py:103
  115.9 122.3 %all-gather.8.cloned.1.call-start = ((), (), s32[]{:S(2)}) async-start(), calls=%async_computation.3 | async-start | bytes 2506752 | tf_op jit(solution)/shard_map/all_gather | solution.py:109
  116.6 402.7 %reduce-scatter.2.cloned.1.call-start = ((), (), s32[]{:S(2)}) async-start(), calls=%async_computation.4 | async-start | bytes 5013504 | tf_op jit(solution)/shard_map/reduce_scatter | solution.py:141
  119.2 118.9 %copy-start.5 = (pred[256]{0:T(512)(128)(4,1)}, pred[256]{0:T(512)(128)(4,1)S(1)}, u32[]{:S(2)}) copy-start(pred[256]{0:T(512)(128)(4,1)S(1)} %add_compare_fusion) | copy-start | bytes 772
  200.6 2.4 copy-start.1
  204.8 37.6 %copy-start.2 = (bf16[256,6,128]{0,2,1:T(8,128)(2,1)}, bf16[256,6,128]{0,2,1:T(8,128)(2,1)S(1)}, u32[]{:S(2)}) copy-start(bf16[256,6,128]{0,2,1:T(8,128)(2,1)S(1)} %fusion.24) | copy-start | bytes 1179652
  243.8 22.7 %collective-permute-start = (bf16[20,1024]{1,0:T(8,128)(2,1)}, bf16[20,1024]{1,0:T(8,128)(2,1)S(1)}, u32[]{:S(2)}, u32[]{:S(2)}) collective-permute-start(bf16[20,1024]{1,0:T(8,128)(2,1)} %get-tuple-element.6), channel_id=1, source_target_pairs={{0,1},{1,2},{2,3},{3,4},{4,5},{5,6},{6,7},{7,8},{8,9},{9,10},{10,1... | collective-permute-start | bytes 122888 | tf_op jit(solution)/shard_map/ppermute | solution.py:19
  246.0 20.6 %collective-permute-start.1 = (bf16[20,1024]{1,0:T(8,128)(2,1)}, bf16[20,1024]{1,0:T(8,128)(2,1)S(1)}, u32[]{:S(2)}, u32[]{:S(2)}) collective-permute-start(bf16[20,1024]{1,0:T(8,128)(2,1)} %get-tuple-element.7), channel_id=1, source_target_pairs={{1,0},{2,1},{3,2},{4,3},{5,4},{6,5},{7,6},{8,7},{9,8},{10,9},{11,1... | collective-permute-start | bytes 122888 | tf_op jit(solution)/shard_map/ppermute | solution.py:20
  277.2 20.1 %copy-start.4 = (f32[1024]{0:T(1024)S(1)}, f32[1024]{0:T(1024)}, u32[]{:S(2)}) copy-start(f32[1024]{0:T(1024)} %param.17) | copy-start | bytes 12292
  299.1 62.8 %collective-permute-start.2 = (bf16[5,1024]{1,0:T(8,128)(2,1)S(1)}, bf16[5,1024]{1,0:T(8,128)(2,1)S(1)}, u32[]{:S(2)}, u32[]{:S(2)}) collective-permute-start(bf16[5,1024]{1,0:T(8,128)(2,1)S(1)} %get-tuple-element.8), channel_id=1, source_target_pairs={{0,1},{1,2},{2,3},{3,4},{4,5},{5,6},{6,7},{7,8},{8,9},{9,10},{10,1... | collective-permute-start | bytes 30728 | tf_op jit(solution)/shard_map/ppermute | solution.py:19
  301.0 60.9 %collective-permute-start.3 = (bf16[5,1024]{1,0:T(8,128)(2,1)S(1)}, bf16[5,1024]{1,0:T(8,128)(2,1)S(1)}, u32[]{:S(2)}, u32[]{:S(2)}) collective-permute-start(bf16[5,1024]{1,0:T(8,128)(2,1)S(1)} %get-tuple-element.9), channel_id=1, source_target_pairs={{1,0},{2,1},{3,2},{4,3},{5,4},{6,5},{7,6},{8,7},{9,8},{10,9},{11,1... | collective-permute-start | bytes 30728 | tf_op jit(solution)/shard_map/ppermute | solution.py:20
  417.8 7.7 %copy-start.3 = (bf16[256,6,128]{0,2,1:T(8,128)(2,1)S(1)}, bf16[256,6,128]{0,2,1:T(8,128)(2,1)}, u32[]{:S(2)}) copy-start(bf16[256,6,128]{0,2,1:T(8,128)(2,1)} %copy-done.2) | copy-start | bytes 1179652
  417.8 7.7 %copy-start.6 = (pred[256]{0:T(512)(128)(4,1)S(1)}, pred[256]{0:T(512)(128)(4,1)}, u32[]{:S(2)}) copy-start(pred[256]{0:T(512)(128)(4,1)} %copy-done.5) | copy-start | bytes 772
  430.4 225.9 %all-reduce.2.cloned.1.call-start = ((), (), s32[]{:S(2)}) async-start(), calls=%async_computation.5 | async-start | bytes 589824 | tf_op jit(solution)/shard_map/psum | solution.py:140
Sparse Core Ops, SparseCore 0:
  10.8 97.2 all-gather.3
  116.0 66.9 all-gather.5
  185.8 52.2 all-gather.7
  430.5 88.7 reduce-scatter.1
  522.0 134.2 all-reduce.1
where the time goes:
time: 678 us; the launch traced here: 666 us
  waiting for transfers between devices  348 us (51%)
  local copies, waits for them, and re-layouts  106 us (16%)
  matrix products  98.3 us (14%)
  blocking collectives  74 us (11%)
  between operations  16.8 us (2%)
  starting transfers between devices  16.1 us (2%)
    all_gather x1, waiting for transfers between devices, shards(): lax.all_gather(kv_weight, 'seq', axis=0, tiled=True)  100 us
    reduce_scatter x1, waiting for transfers between devices, shards(): lax.psum_scatter(summed_clips, 'seq', scatter_dimension=0, tiled=True)  88.9 us
    psum x1, blocking collectives, shards(): total_loss = lax.psum(local_loss, ('dp', 'seq'))  74 us
    all_gather x1, waiting for transfers between devices, shards(): keys_values = lax.all_gather(projected, 'seq', axis=0, tiled=True)  63.1 us
    psum x1, waiting for transfers between devices, shards(): summed_clips = lax.psum(full_term, 'dp')  61.6 us
    conv_general_dilated x1, matrix products, disc_back(): lax.conv_general_dilated(grad_wide[None], flipped, (1,), [(0, high_pad)],...  54.6 us
    another operation x2, local copies, waits for them, and re-layouts  33.9 us
    all_gather x1, waiting for transfers between devices, shards(): lax.all_gather(out_proj, 'seq', axis=0, tiled=True)  33.3 us
  transfers between devices with their start and end apart: 9, of which 5 were waited for; matrix products, arithmetic and copies ran while one was open for 14% of the time, Pallas kernels for 0%

commit v1 on v0

--- a/solution.py
+++ b/solution.py
@@ -97,7 +97,9 @@
     sliced = states_local
     projected = jnp.dot(
         sliced,
-        lax.all_gather(kv_weight, "seq", axis=0, tiled=True),
+        jnp.concatenate(
+            lax.all_to_all(jnp.stack([kv_weight] * lax.axis_size("seq")), "seq", 0, 0), axis=0
+        ),
         preferred_element_type=jnp.float32,
     )
     keys_values = lax.all_gather(projected, "seq", axis=0, tiled=True)

time: 678 us -> 720 us (1.062)
  blocking collectives: 74 us -> 221 us
  waiting for transfers between devices: 348 us -> 252 us
    all_to_all x0 -> x1, blocking collectives: none -> 147 us  [shards(): lax.all_to_all(jnp.stack([kv_weight] * lax.axis_size('seq')), 'seq', 0, 0)]
    all_gather x1 -> x0, waiting for transfers between devices: 100 us -> none  [shards(): lax.all_gather(kv_weight, 'seq', axis=0, tiled=True)]
    another operation x2 -> x3, local copies, waits for them, and re-layouts: 33.9 us -> 40.9 us
  transfers between devices with their start and end apart: 9 -> 8, of which waited for: 5 -> 4; matrix products, arithmetic and copies ran while one was open for 14% -> 13% of each run, Pallas kernels for 0% -> 0%
where the time goes in v1:
time: 720 us; the launch traced here: 715 us
  waiting for transfers between devices  252 us (35%)
  blocking collectives  221 us (31%)
  local copies, waits for them, and re-layouts  113 us (16%)
  matrix products  93.5 us (13%)
  between operations  16.6 us (2%)
  starting transfers between devices  13.1 us (2%)
    all_to_all x1, blocking collectives, shards(): lax.all_to_all(jnp.stack([kv_weight] * lax.axis_size('seq')), 'seq', 0, 0)  147 us
    reduce_scatter x1, waiting for transfers between devices, shards(): lax.psum_scatter(summed_clips, 'seq', scatter_dimension=0, tiled=True)  92 us
    psum x1, blocking collectives, shards(): total_loss = lax.psum(local_loss, ('dp', 'seq'))  74 us
    all_gather x1, waiting for transfers between devices, shards(): keys_values = lax.all_gather(projected, 'seq', axis=0, tiled=True)  64.4 us
    psum x1, waiting for transfers between devices, shards(): summed_clips = lax.psum(full_term, 'dp')  61.6 us
    conv_general_dilated x1, matrix products, disc_back(): lax.conv_general_dilated(grad_wide[None], flipped, (1,), [(0, high_pad)],...  54.6 us
    another operation x2, local copies, waits for them, and re-layouts  33.9 us
    all_gather x1, waiting for transfers between devices, shards(): lax.all_gather(out_proj, 'seq', axis=0, tiled=True)  33.3 us
  transfers between devices with their start and end apart: 8, of which 4 were waited for; matrix products, arithmetic and copies ran while one was open for 13% of the time, Pallas kernels for 0%

profile of v1, /device:TPU:8, one launch (start us, length us, event | category | flops | bytes accessed | tf_op | source)
XLA Modules:
  0.0 715.1 jit_solution(16003585780314225475)
XLA Ops:
  7.2 0.0 copy-start
  7.2 0.0 all-gather.3.cloned.1.call-start
  7.2 7.1 stack.2
  14.3 146.5 %all_to_all.5 = bf16[16,256,1536]{2,1,0:T(8,128)(2,1)S(1)} all-to-all(bf16[16,256,1536]{2,1,0:T(8,128)(2,1)} %stack.2), channel_id=1, replica_groups=mesh['dp'=16,'seq'=16] {'seq'}, dimensions={0} | all-to-all | bytes 25165824 | tf_op jit(solution)/shard_map/all_to_all | solution.py:101
  160.8 0.0 copy-done.4
  160.8 3.0 fusion.31
  163.8 0.0 all-gather.3.cloned.1.call-update
  163.8 0.0 all-gather.5.cloned.1.call-start
  163.9 0.7 all-gather.5.cloned.1.call-update
  164.6 0.5 reduce-scatter.2.cloned.1.call-start
  165.1 1.2 copy.20
  166.3 0.0 copy-done.8
  166.3 0.0 copy-done.9
  166.3 0.7 fusion.42
  167.0 0.7 add_compare_fusion
  167.7 0.0 copy-start.6
  167.7 0.7 iota_compare_fusion
  168.4 64.4 %all-gather.3.cloned.1.call-done = f32[1024,1536]{1,0:T(8,128)} async-done(((f32[64,1536]{1,0:T(8,128)}), f32[1024,1536]{1,0:T(8,128)}) %all-gather.3.cloned.1.call-update) | async-done | bytes 6291472 | tf_op jit(solution)/shard_map/all_gather | solution.py:105
  232.7 5.9 fusion.48
  238.6 3.5 copy.18
  242.2 3.6 copy.19
  245.7 4.6 fusion.52
  250.4 0.0 copy-start.1
  250.4 2.4 fusion.51
  252.8 0.0 copy-done.1
  252.8 1.7 fusion.24
  254.5 0.0 copy-start.2
  254.5 33.3 %all-gather.5.cloned.1.call-done = bf16[768,1536]{1,0:T(8,128)(2,1)} async-done(((bf16[48,1536]{1,0:T(8,128)(2,1)}), bf16[768,1536]{1,0:T(8,128)(2,1)}) %all-gather.5.cloned.1.call-update) | async-done | bytes 2359312 | tf_op jit(solution)/shard_map/all_gather | solution.py:111
  287.8 4.3 fusion.23
  292.1 0.0 copy-done.2
  292.1 1.5 fusion.49
  293.6 2.6 collective-permute-start.1
  296.1 1.9 collective-permute-start
  298.1 14.8 %shard_map.115 = bf16[41,64,16,64]{3,2,1,0:T(8,128)(2,1)} reshape(bf16[41,64,1024]{2,1,0:T(8,128)(2,1)} %param.16) | data formatting | bytes 10747904 | tf_op jit(solution)/shard_map/shard_map
  312.8 0.0 collective-permute-done.1
  312.8 0.0 collective-permute-done
  312.8 2.0 pad_maximum_fusion
  314.9 2.3 copy.24
  317.1 6.3 copy.25
  323.5 0.0 copy-start.5
  323.5 18.9 %fusion.27 = f32[64,16,64]{2,1,0:T(8,128)} fusion(bf16[1,296,16,64]{3,0,2,1:T(2,128)(2,1)} %copy.25, bf16[41,64,16,64]{3,2,1,0:T(8,128)(2,1)} %shard_map.115), kind=kOutput, calls=%fused_computation.25 | convolution fusion | flops 343932928 | bytes 6242304 | tf_op jit(solution)/shard_map/conv_general_dilated | solution.py:33
  342.4 1.2 squeeze.12
  343.5 1.7 fusion.41
  345.2 0.1 multiply_convert_fusion
  345.3 6.0 collective-permute-start.3
  351.4 1.9 collective-permute-start.2
  353.3 19.1 %copy.27 = bf16[41,64,16,64]{1,2,3,0:T(8,128)(2,1)} copy(bf16[41,64,16,64]{3,2,1,0:T(8,128)(2,1)} %shard_map.115) | data formatting | bytes 10747904 | tf_op jit(solution)/shard_map/shard_map
  372.4 15.0 %reshape.54 = bf16[41,64,1024]{2,1,0:T(8,128)(2,1)} reshape(bf16[41,64,16,64]{3,2,1,0:T(8,128)(2,1)} %bitcast.57) | data formatting | bytes 10747904 | tf_op jit(solution)/shard_map/reshape | solution.py:28
  387.5 5.9 rev.6
  393.4 14.8 %rev.7 = bf16[41,64,16,64]{3,2,1,0:T(8,128)(2,1)} reshape(bf16[41,64,1024]{2,1,0:T(8,128)(2,1)} %rev.6) | data formatting | bytes 10747904 | tf_op jit(solution)/shard_map/jit(_flip)/rev | solution.py:29
  408.2 0.0 collective-permute-done.3
  408.2 0.0 collective-permute-done.2
  408.2 1.2 broadcast_in_dim.69
  409.4 54.6 %fusion.1 = bf16[1,256,16,64]{3,0,2,1:T(2,128)(2,1)} fusion(bf16[1,74,16,64]{3,0,2,1:T(2,128)(2,1)} %broadcast_in_dim.69, bf16[41,64,16,64]{3,2,1,0:T(8,128)(2,1)} %rev.7), kind=kOutput, calls=%fused_computation.1 | convolution fusion | flops 343932928 | bytes 6049792 | tf_op jit(solution)/shard_map/conv_general_dilated | solution.py:45
  464.0 5.7 copy.30
  469.7 2.1 copy.31
  471.8 4.8 fusion.16
  476.5 0.0 reduce-scatter.2.cloned.1.call-update
  476.6 0.0 all-reduce.2.cloned.1.call-start
  476.6 92.0 %reduce-scatter.2.cloned.1.call-done = f32[48,1536]{1,0:T(8,128)} async-done(((f32[768,1536]{1,0:T(8,128)}), f32[48,1536]{1,0:T(8,128)}) %reduce-scatter.2.cloned.1.call-update) | async-done | bytes 294928 | tf_op jit(solution)/shard_map/reduce_scatter | solution.py:143
  568.6 0.0 all-reduce.2.cloned.1.call-update
  569.2 74.0 %psum.15 = f32[]{:T(128)} all-reduce(f32[]{:T(128)} %get-tuple-element.10), channel_id=1, replica_groups=mesh['dp'=16,'seq'=16] {'dp','seq'}, use_global_device_ids=true, to_apply=%region_7.8 | all-reduce | flops 1 | bytes 8 | tf_op jit(solution)/shard_map/psum | solution.py:144
  643.9 61.6 %all-reduce.2.cloned.1.call-done = f32[48,1536]{1,0:T(8,128)} async-done(((f32[48,1536]{1,0:T(8,128)}), f32[48,1536]{1,0:T(8,128)}) %all-reduce.2.cloned.1.call-update) | async-done | bytes 294928 | tf_op jit(solution)/shard_map/psum | solution.py:142
  705.5 1.7 copy.42
  (12 shorter events, 0.1 us)
Async XLA Ops:
  7.2 280.7 %copy-start = (bf16[1536,1024]{1,0:T(8,128)(2,1)S(1)}, bf16[1536,1024]{1,0:T(8,128)(2,1)}, u32[]{:S(2)}) copy-start(bf16[1536,1024]{1,0:T(8,128)(2,1)} %param.15) | copy-start | bytes 9437188
  7.2 225.6 %all-gather.3.cloned.1.call-start = ((), (), s32[]{:S(2)}) async-start(), calls=%async_computation.2 | async-start | bytes 6684672 | tf_op jit(solution)/shard_map/all_gather | solution.py:105
  14.3 146.5 %copy-start.4 = (bf16[1,64,4096]{2,1,0:T(8,128)(2,1)S(1)}, bf16[1,64,4096]{2,1,0:T(8,128)(2,1)}, u32[]{:S(2)}) copy-start(bf16[1,64,4096]{2,1,0:T(8,128)(2,1)} %param.10) | copy-start | bytes 1572868
  160.8 5.5 copy-start.8
  160.8 5.5 copy-start.9
  163.8 124.0 %all-gather.5.cloned.1.call-start = ((), (), s32[]{:S(2)}) async-start(), calls=%async_computation.3 | async-start | bytes 2506752 | tf_op jit(solution)/shard_map/all_gather | solution.py:111
  164.6 404.0 %reduce-scatter.2.cloned.1.call-start = ((), (), s32[]{:S(2)}) async-start(), calls=%async_computation.4 | async-start | bytes 5013504 | tf_op jit(solution)/shard_map/reduce_scatter | solution.py:143
  167.7 120.1 %copy-start.6 = (pred[256]{0:T(512)(128)(4,1)}, pred[256]{0:T(512)(128)(4,1)S(1)}, u32[]{:S(2)}) copy-start(pred[256]{0:T(512)(128)(4,1)S(1)} %add_compare_fusion) | copy-start | bytes 772
  250.4 2.4 copy-start.1
  254.5 37.6 %copy-start.2 = (bf16[256,6,128]{0,2,1:T(8,128)(2,1)}, bf16[256,6,128]{0,2,1:T(8,128)(2,1)S(1)}, u32[]{:S(2)}) copy-start(bf16[256,6,128]{0,2,1:T(8,128)(2,1)S(1)} %fusion.24) | copy-start | bytes 1179652
  293.6 19.3 %collective-permute-start.1 = (bf16[20,1024]{1,0:T(8,128)(2,1)}, bf16[20,1024]{1,0:T(8,128)(2,1)S(1)}, u32[]{:S(2)}, u32[]{:S(2)}) collective-permute-start(bf16[20,1024]{1,0:T(8,128)(2,1)} %get-tuple-element.7), channel_id=1, source_target_pairs={{1,0},{2,1},{3,2},{4,3},{5,4},{6,5},{7,6},{8,7},{9,8},{10,9},{11,1... | collective-permute-start | bytes 122888 | tf_op jit(solution)/shard_map/ppermute | solution.py:20
  296.1 16.7 %collective-permute-start = (bf16[20,1024]{1,0:T(8,128)(2,1)}, bf16[20,1024]{1,0:T(8,128)(2,1)S(1)}, u32[]{:S(2)}, u32[]{:S(2)}) collective-permute-start(bf16[20,1024]{1,0:T(8,128)(2,1)} %get-tuple-element.6), channel_id=1, source_target_pairs={{0,1},{1,2},{2,3},{3,4},{4,5},{5,6},{6,7},{7,8},{8,9},{9,10},{10,1... | collective-permute-start | bytes 122888 | tf_op jit(solution)/shard_map/ppermute | solution.py:19
  323.5 20.1 %copy-start.5 = (f32[1024]{0:T(1024)S(1)}, f32[1024]{0:T(1024)}, u32[]{:S(2)}) copy-start(f32[1024]{0:T(1024)} %param.17) | copy-start | bytes 12292
  345.3 62.8 %collective-permute-start.3 = (bf16[5,1024]{1,0:T(8,128)(2,1)S(1)}, bf16[5,1024]{1,0:T(8,128)(2,1)S(1)}, u32[]{:S(2)}, u32[]{:S(2)}) collective-permute-start(bf16[5,1024]{1,0:T(8,128)(2,1)S(1)} %get-tuple-element.9), channel_id=1, source_target_pairs={{1,0},{2,1},{3,2},{4,3},{5,4},{6,5},{7,6},{8,7},{9,8},{10,9},{11,1... | collective-permute-start | bytes 30728 | tf_op jit(solution)/shard_map/ppermute | solution.py:20
  351.4 56.8 %collective-permute-start.2 = (bf16[5,1024]{1,0:T(8,128)(2,1)S(1)}, bf16[5,1024]{1,0:T(8,128)(2,1)S(1)}, u32[]{:S(2)}, u32[]{:S(2)}) collective-permute-start(bf16[5,1024]{1,0:T(8,128)(2,1)S(1)} %get-tuple-element.8), channel_id=1, source_target_pairs={{0,1},{1,2},{2,3},{3,4},{4,5},{5,6},{6,7},{7,8},{8,9},{9,10},{10,1... | collective-permute-start | bytes 30728 | tf_op jit(solution)/shard_map/ppermute | solution.py:19
  464.0 7.7 %copy-start.3 = (bf16[256,6,128]{0,2,1:T(8,128)(2,1)S(1)}, bf16[256,6,128]{0,2,1:T(8,128)(2,1)}, u32[]{:S(2)}) copy-start(bf16[256,6,128]{0,2,1:T(8,128)(2,1)} %copy-done.2) | copy-start | bytes 1179652
  464.0 7.7 %copy-start.7 = (pred[256]{0:T(512)(128)(4,1)S(1)}, pred[256]{0:T(512)(128)(4,1)}, u32[]{:S(2)}) copy-start(pred[256]{0:T(512)(128)(4,1)} %copy-done.6) | copy-start | bytes 772
  476.6 228.9 %all-reduce.2.cloned.1.call-start = ((), (), s32[]{:S(2)}) async-start(), calls=%async_computation.5 | async-start | bytes 589824 | tf_op jit(solution)/shard_map/psum | solution.py:142
Sparse Core Ops, SparseCore 0:
  163.9 68.7 all-gather.2
  235.5 52.2 all-gather.4
  476.7 91.8 reduce-scatter.1
  571.2 134.1 all-reduce.1
